TPU v7x, 256 devices: a whole 4x4x8 slice. The times are simulated.
256 devices in a mesh: grp: 2 (over core), seq: 16 (over y, x), tp: 8 (over z).
Axes of the slice: x: 4, y: 4, z: 8, core: 2. Of those that a mesh axis runs over, the one named last changes fastest.
Arguments:
- prompt: bfloat16 [16384, 8192], P(('grp', 'seq'), 'tp'), may hold values from -6 to 6
- w_kv: bfloat16 [8192, 2048], P(None, 'tp'), may hold values from -0.0625 to 0.0625
- block_owner: int32 [2048, 1], P(('grp', 'seq')), may hold values from 0 to 31, as said below
- block_row: int32 [2048], P(('grp', 'seq')), may hold values from 0 to 31, as said below
- queries: bfloat16 [1024, 4, 8192], P(('grp', 'seq'), None, 'tp'), may hold values from -150 to 150
- new_kv: bfloat16 [1024, 4, 2048], P(('grp', 'seq'), None, 'tp'), may hold values from -6 to 6
- cache_codes: bfloat16 [1024, 128, 2048], P(('grp', 'seq'), None, 'tp'), may hold values from -4 to 4
- cache_scales: float32 [1024, 8, 16], P(('grp', 'seq'), None, 'tp'), may hold values from 0.5 to 2
- lengths: int32 [1024], P(('grp', 'seq')), may hold values from 1 to 128, 65536 in all
- w_out: bfloat16 [8192, 8192], P('tp', 'seq'), may hold values from -0.5 to 0.5
Outputs:
- mixed: bfloat16 [4096, 8192], P(('grp', 'tp'), 'seq')
Inputs may be any that keep to these rules, and one draw needn't show every extreme that they name: `block_owner`: the blocks come in aligned groups of 8 consecutive blocks that share one owner and one request; the groups of one prefill device all go to different owners, so a prefill device sends exactly 8 blocks to each owner it sends to. `block_row`: equal on all blocks of one aligned group of 8 blocks.
All inputs are finite; a program needn't handle non-finite values. No bound on the sum of `lengths` on one device may be relied on, other than what follows from the above.
Results may differ from a plain program's by a relative error of at most 0.014.
Values may be sent and summed in bfloat16 or wider, within the bound.
No kernel may reach another device: no remote copies, remote signals or barrier semaphores. Data moves between devices by JAX's collectives and lax.ppermute only.
A program may use at most 256 MiB of HBM per device.

v0:
```python
import math
import jax
import jax.numpy as jnp
from jax import lax
from jax.sharding import PartitionSpec as P

HQ = 64
KVH = 8
HD = 128
NEW = 4
BLK = 8
CBLK = 16
CAP = 8
EPS = 1e-05


def on_device(
    prompt, w_kv, block_owner, block_row, queries, new_kv, cache_codes, cache_scales, lengths, w_out
):
    group_count = lax.axis_size("grp")
    seq_count = lax.axis_size("seq")
    owners = group_count * seq_count
    tokens = prompt.shape[0]
    features = w_kv.shape[0]
    columns = w_kv.shape[1]
    row_count = queries.shape[0]
    shard_piece = lax.all_gather(prompt, "tp", axis=1, tiled=True)
    running = jnp.dot(shard_piece, w_kv, preferred_element_type=jnp.float32)
    widened = shard_piece.astype(jnp.float32)
    squares = jnp.sum(widened * widened, axis=1)
    row_scale = lax.rsqrt(squares / features + EPS)
    prompt_kv = (running * row_scale[:, None]).astype(jnp.bfloat16)
    blocks = tokens // BLK
    capacity = CAP
    owner_ids = block_owner[:, 0]
    owner_onehot = (owner_ids[:, None] == jnp.arange(owners, dtype=jnp.int32)[None, :]).astype(
        jnp.int32
    )
    slot_rank = jnp.sum((jnp.cumsum(owner_onehot, axis=0) - owner_onehot) * owner_onehot, axis=1)
    target = owner_ids * capacity + slot_rank
    chosen = target[None, :] == jnp.arange(owners * capacity, dtype=jnp.int32)[:, None]
    packed = jnp.dot(
        chosen.astype(jnp.bfloat16),
        prompt_kv.reshape(blocks, BLK * columns),
        preferred_element_type=jnp.float32,
    )
    send_kv = packed.astype(jnp.bfloat16).reshape(owners, capacity, BLK, columns)
    send_rows = (jnp.sum(jnp.where(chosen, block_row[None, :] + 1, 0), axis=1) - 1).reshape(
        owners, capacity
    )
    arrived_kv, arrived_rows = (
        lax.all_to_all(send_kv, ("grp", "seq"), split_axis=0, concat_axis=0, tiled=True),
        lax.all_to_all(send_rows, ("grp", "seq"), split_axis=0, concat_axis=0, tiled=True),
    )
    slots = arrived_rows.shape[1]
    kv_heads = columns // (2 * HD)
    head_group = HQ // KVH
    context = cache_codes.shape[1]
    query_heads = queries.reshape(row_count, NEW, kv_heads, head_group, HD)
    fresh_kv = new_kv.reshape(row_count, NEW, kv_heads, 2, HD)
    stored = cache_codes.reshape(row_count, context, kv_heads, 2, HD)
    block_scales = cache_scales.reshape(row_count, context // CBLK, kv_heads, 2)
    key_scale = jnp.transpose(jnp.repeat(block_scales[:, :, :, 0], CBLK, axis=1), (0, 2, 1))
    value_scale = jnp.transpose(jnp.repeat(block_scales[:, :, :, 1], CBLK, axis=1), (0, 2, 1))
    arrived = arrived_kv.reshape(owners * slots * BLK, kv_heads, 2, HD)
    arrived_targets = jnp.broadcast_to(arrived_rows[:, :, None], (owners, slots, BLK)).reshape(
        owners * slots * BLK
    )
    inverse_root = 1.0 / math.sqrt(HD)
    row_ids = jnp.arange(row_count, dtype=jnp.int32)
    s_cache = jnp.einsum(
        "rinhd,rpnd->rinhp", query_heads, stored[:, :, :, 0, :], preferred_element_type=jnp.float32
    )
    s_cache = s_cache * key_scale[:, None, :, None, :] * inverse_root
    cache_live = jnp.arange(context, dtype=jnp.int32)[None, :] < lengths[:, None]
    s_cache = jnp.where(cache_live[:, None, None, None, :], s_cache, -jnp.inf)
    s_sent = (
        jnp.einsum(
            "rinhd,knd->rinhk", query_heads, arrived[:, :, 0, :], preferred_element_type=jnp.float32
        )
        * inverse_root
    )
    sent_live = arrived_targets[None, :] == row_ids[:, None]
    s_sent = jnp.where(sent_live[:, None, None, None, :], s_sent, -jnp.inf)
    s_fresh = (
        jnp.einsum(
            "rinhd,rjnd->rinhj",
            query_heads,
            fresh_kv[:, :, :, 0, :],
            preferred_element_type=jnp.float32,
        )
        * inverse_root
    )
    causal = jnp.arange(NEW)[None, :] <= jnp.arange(NEW)[:, None]
    s_fresh = jnp.where(causal[None, :, None, None, :], s_fresh, -jnp.inf)
    row_max = jnp.maximum(
        jnp.maximum(jnp.max(s_cache, axis=-1), jnp.max(s_sent, axis=-1)), jnp.max(s_fresh, axis=-1)
    )
    w_cache = jnp.exp(s_cache - row_max[..., None])
    w_sent = jnp.exp(s_sent - row_max[..., None])
    w_fresh = jnp.exp(s_fresh - row_max[..., None])
    denominator = jnp.sum(w_cache, axis=-1) + jnp.sum(w_sent, axis=-1) + jnp.sum(w_fresh, axis=-1)
    cache_weights = (w_cache * value_scale[:, None, :, None, :]).astype(jnp.bfloat16)
    numerator = jnp.einsum(
        "rinhp,rpnd->rinhd",
        cache_weights,
        stored[:, :, :, 1, :],
        preferred_element_type=jnp.float32,
    )
    numerator = numerator + jnp.einsum(
        "rinhk,knd->rinhd",
        w_sent.astype(jnp.bfloat16),
        arrived[:, :, 1, :],
        preferred_element_type=jnp.float32,
    )
    numerator = numerator + jnp.einsum(
        "rinhj,rjnd->rinhd",
        w_fresh.astype(jnp.bfloat16),
        fresh_kv[:, :, :, 1, :],
        preferred_element_type=jnp.float32,
    )
    attention = (
        (numerator / denominator[..., None])
        .astype(jnp.bfloat16)
        .reshape(row_count * NEW, kv_heads * head_group * HD)
    )
    head_terms = jnp.dot(
        lax.all_gather(attention, "seq", axis=0, tiled=True),
        w_out,
        preferred_element_type=jnp.float32,
    )
    return lax.psum_scatter(head_terms.astype(jnp.bfloat16), "tp", scatter_dimension=0, tiled=True)


def solution(mesh):
    in_specs = (
        P(("grp", "seq"), "tp"),
        P(None, "tp"),
        P(("grp", "seq"), None),
        P(("grp", "seq")),
        P(("grp", "seq"), None, "tp"),
        P(("grp", "seq"), None, "tp"),
        P(("grp", "seq"), None, "tp"),
        P(("grp", "seq"), None, "tp"),
        P(("grp", "seq")),
        P("tp", "seq"),
    )
    out_specs = P(("grp", "tp"), "seq")
    return jax.shard_map(
        on_device, mesh=mesh, in_specs=in_specs, out_specs=out_specs, check_vma=False
    )
```

profile of v0, /device:TPU:2, one launch (start us, length us, event | category | flops | bytes accessed | tf_op | source)
XLA Modules:
  0.0 270.8 jit_solution(4735549890900812305)
XLA Ops:
  6.6 0.7 all-gather.3.cloned.1.call-update
  7.3 0.7 fusion.33
  8.1 0.8 select_reduce_fusion.1
  10.4 0.7 sub.35
  11.1 7.6 %all-to-all-start = ((s32[32,1,8]{2,1,0:T(1,128)}), s32[32,1,8]{2,1,0:T(1,128)S(1)}, u32[]{:S(2)}, u32[]{:S(2)}) async-start(s32[32,1,8]{2,1,0:T(1,128)} %bitcast.10), calls=%async_computation | async-start | bytes 32768 | tf_op jit(solution)/shard_map/all_to_all | solution.py:53
  18.7 1.1 reshape.223
  19.8 4.1 %copy.64 = bf16[32,128,256]{1,2,0:T(8,128)(2,1)} copy(bf16[32,128,256]{2,1,0:T(8,128)(2,1)} %param.16) | data formatting | bytes 4194304 | tf_op args[6]
  24.2 82.0 %all-gather.3.cloned.1.call-done = bf16[512,8192]{1,0:T(8,128)(2,1)} async-done(((bf16[512,1024]{1,0:T(8,128)(2,1)}), bf16[512,8192]{1,0:T(8,128)(2,1)}) %all-gather.3.cloned.1.call-update) | async-done | bytes 8388624 | tf_op jit(solution)/shard_map/all_gather | solution.py:27
  106.2 5.3 %multiply_reduce_fusion = f32[512]{0:T(512)S(1)} fusion(bf16[512,8192]{1,0:T(8,128)(2,1)} %all-gather.3.cloned.1.call-done), kind=kLoop, calls=%fused_computation | loop fusion | flops 12582400 | bytes 8390656 | tf_op jit(solution)/shard_map/reduce_sum | solution.py:30
  112.0 4.6 %fusion.16 = bf16[512,256]{1,0:T(8,128)(2,1)S(1)} fusion(bf16[512,8192]{1,0:T(8,128)(2,1)S(1)} %copy-done.1, bf16[8192,256]{1,0:T(8,128)(2,1)} %param.11, f32[512]{0:T(512)S(1)} %add_rsqrt_fusion), kind=kOutput, calls=%fused_computation.23 | convolution fusion | flops 2147745792 | bytes 12847104 | tf_op jit(solution)/shard_map/dot_general | solution.py:28
  117.2 1.3 copy.68
  118.5 7.4 %all-to-all-start.1 = ((bf16[32,8,8,256]{3,2,1,0:T(8,128)(2,1)}), bf16[32,8,8,256]{3,2,1,0:T(8,128)(2,1)S(1)}, u32[]{:S(2)}, u32[]{:S(2)}) async-start(bf16[32,8,8,256]{3,2,1,0:T(8,128)(2,1)} %copy.68), calls=%async_computation.1 | async-start | bytes 2097152 | tf_op jit(solution)/shard_map/all_to_all | solution.py:52
  126.2 2.6 fusion.37
  128.8 3.0 %fusion.38 = (f32[32,4,8]{2,1,0:T(4,128)}, f32[32,4,1,8,128]{4,3,1,0,2:T(8,128)}) fusion(f32[32,128]{1,0:T(8,128)S(1)} %copy.66, bf16[32,4,8,128]{3,2,1,0:T(8,128)(2,1)S(1)} %reshape.223, bf16[32,128,1,2,128]{1,4,3,0,2:T(8,128)(2,1)} %bitcast.147, pred[32,128]{1,0:T(8,128)(4,1)S(1)} %iota_compare_fusion.4), kind=kOutput, calls=%fused_computation.67 | convolution fusion | flops 34077696 | bytes 1859584 | tf_op jit(solution)/shard_map/rinhd,rpnd->rinhp/dot_general | solution.py:71
  132.1 9.2 %all-to-all-done.1 = bf16[32,8,8,256]{3,2,1,0:T(8,128)(2,1)S(1)} async-done(((bf16[32,8,8,256]{3,2,1,0:T(8,128)(2,1)}), bf16[32,8,8,256]{3,2,1,0:T(8,128)(2,1)S(1)}, u32[]{:S(2)}, u32[]{:S(2)}) %all-to-all-start.1) | async-done | bytes 1048608 | tf_op jit(solution)/shard_map/all_to_all | solution.py:52
  141.5 2.3 fusion.34
  143.9 4.6 %fusion.2 = (f32[32,4,8]{0,2,1:T(8,128)S(1)}, f32[2048,32,4,8]{0,1,3,2:T(8,128)}) fusion(pred[32,2048]{1,0:T(8,128)(4,1)S(1)} %iota_compare_fusion, bf16[32,4,8,128]{3,2,1,0:T(8,128)(2,1)S(1)} %reshape.223, bf16[2048,1,1,128]{3,2,0,1:T(2,128)(2,1)S(1)} %get-tuple-element.8), kind=kOutput, calls=%fused_computation.5 | convolution fusion | flops 543161344 | bytes 9244672 | tf_op jit(solution)/shard_map/rinhd,knd->rinhk/dot_general | solution.py:78
  148.6 5.9 %fusion = (f32[32,4,8]{0,2,1:T(8,128)S(1)}, bf16[32,4,8,2048]{3,0,2,1:T(8,128)(2,1)}) fusion(f32[2048,32,4,8]{0,1,3,2:T(8,128)} %get-tuple-element.18, f32[32,4,8]{0,2,1:T(8,128)S(1)} %copy.77, pred[32,2048]{1,0:T(8,128)(4,1)S(1)} %iota_compare_fusion), kind=kLoop, calls=%fused_computation.3 | loop fusion | flops 10484736 | bytes 12656640 | tf_op jit(solution)/shard_map/reduce_sum | solution.py:102
  155.6 5.1 %fusion.13 = f32[32,4,1,8,128]{4,3,1,0,2:T(8,128)S(1)} fusion(bf16[32,4,8,2048]{3,0,2,1:T(8,128)(2,1)} %get-tuple-element.6, bf16[2048,1,1,128]{3,2,0,1:T(2,128)(2,1)S(1)} %copy-done.4), kind=kOutput, calls=%fused_computation.21 | convolution fusion | flops 536870912 | bytes 5242880 | tf_op jit(solution)/shard_map/rinhk,knd->rinhd/dot_general | solution.py:110
  160.8 0.7 fusion.17
  161.5 0.8 copy.120
  162.3 53.3 %all-gather.5.cloned.1.call-done = bf16[2048,1024]{1,0:T(8,128)(2,1)} async-done(((bf16[128,1024]{1,0:T(8,128)(2,1)}), bf16[2048,1024]{1,0:T(8,128)(2,1)}) %all-gather.5.cloned.1.call-update) | async-done | bytes 4194320 | tf_op jit(solution)/shard_map/all_gather | solution.py:128
  215.7 5.9 %convolution_convert_fusion = bf16[2048,512]{1,0:T(8,128)(2,1)} fusion(bf16[2048,1024]{1,0:T(8,128)(2,1)} %all-gather.5.cloned.1.call-done, bf16[1024,512]{1,0:T(8,128)(2,1)S(1)} %copy-done), kind=kOutput, calls=%fused_computation.9 | convolution fusion | flops 2148532224 | bytes 7340032 | tf_op jit(solution)/shard_map/dot_general | solution.py:127
  221.5 42.8 %reduce-scatter.2.cloned.1.call-done = bf16[256,512]{1,0:T(8,128)(2,1)} async-done(((bf16[2048,512]{1,0:T(8,128)(2,1)}), bf16[256,512]{1,0:T(8,128)(2,1)}) %reduce-scatter.2.cloned.1.call-update) | async-done | bytes 262160 | tf_op jit(solution)/shard_map/reduce_scatter | solution.py:132
  (57 shorter events, 5.2 us)
Async XLA Ops:
  6.5 209.1 %copy-start = (bf16[1024,512]{1,0:T(8,128)(2,1)S(1)}, bf16[1024,512]{1,0:T(8,128)(2,1)}, u32[]{:S(2)}) copy-start(bf16[1024,512]{1,0:T(8,128)(2,1)} %param.19) | copy-start | bytes 3145732
  6.5 17.3 %copy-start.9 = (f32[32,8,2]{0,2,1:T(2,128)S(1)}, f32[32,8,2]{0,2,1:T(2,128)}, u32[]{:S(2)}) copy-start(f32[32,8,2]{0,2,1:T(2,128)} %param.17) | copy-start | bytes 6148
  6.5 17.4 %copy-start.6 = (bf16[32,4,256]{2,1,0:T(4,128)(2,1)S(1)}, bf16[32,4,256]{2,1,0:T(4,128)(2,1)}, u32[]{:S(2)}) copy-start(bf16[32,4,256]{2,1,0:T(4,128)(2,1)} %param.15) | copy-start | bytes 196612
  6.5 17.5 %copy-start.10 = (s32[32]{0:T(128)S(1)}, s32[32]{0:T(128)}, u32[]{:S(2)}) copy-start(s32[32]{0:T(128)} %param.18) | copy-start | bytes 388
  6.5 99.7 %all-gather.3.cloned.1.call-start = ((), (), s32[]{:S(2)}) async-start(), calls=%async_computation.3 | async-start | bytes 9437184 | tf_op jit(solution)/shard_map/all_gather | solution.py:27
  11.1 107.4 %all-to-all-start = ((s32[32,1,8]{2,1,0:T(1,128)}), s32[32,1,8]{2,1,0:T(1,128)S(1)}, u32[]{:S(2)}, u32[]{:S(2)}) async-start(s32[32,1,8]{2,1,0:T(1,128)} %bitcast.10), calls=%async_computation | async-start | bytes 32768 | tf_op jit(solution)/shard_map/all_to_all | solution.py:53
  106.2 5.8 %copy-start.1 = (bf16[512,8192]{1,0:T(8,128)(2,1)S(1)}, bf16[512,8192]{1,0:T(8,128)(2,1)}, u32[]{:S(2)}) copy-start(bf16[512,8192]{1,0:T(8,128)(2,1)} %all-gather.3.cloned.1.call-done) | copy-start | bytes 25165828
  118.5 22.8 %all-to-all-start.1 = ((bf16[32,8,8,256]{3,2,1,0:T(8,128)(2,1)}), bf16[32,8,8,256]{3,2,1,0:T(8,128)(2,1)S(1)}, u32[]{:S(2)}, u32[]{:S(2)}) async-start(bf16[32,8,8,256]{3,2,1,0:T(8,128)(2,1)} %copy.68), calls=%async_computation.1 | async-start | bytes 2097152 | tf_op jit(solution)/shard_map/all_to_all | solution.py:52
  125.9 89.7 %all-gather.5.cloned.1.call-start = ((), (), s32[]{:S(2)}) async-start(), calls=%async_computation.4 | async-start | bytes 4456448 | tf_op jit(solution)/shard_map/all_gather | solution.py:128
  143.8 4.7 %copy-start.7 = (f32[32,4,8]{2,1,0:T(4,128)S(1)}, f32[32,4,8]{2,1,0:T(4,128)}, u32[]{:S(2)}) copy-start(f32[32,4,8]{2,1,0:T(4,128)} %get-tuple-element.13) | copy-start | bytes 12292
  143.9 4.7 %copy-start.8 = (f32[32,4,8]{2,1,0:T(4,128)S(1)}, f32[32,4,8]{2,1,0:T(4,128)}, u32[]{:S(2)}) copy-start(f32[32,4,8]{2,1,0:T(4,128)} %get-tuple-element.15) | copy-start | bytes 12292
  148.6 6.0 %copy-start.5 = (f32[32,4,1,8,128]{4,3,1,0,2:T(8,128)S(1)}, f32[32,4,1,8,128]{4,3,1,0,2:T(8,128)}, u32[]{:S(2)}) copy-start(f32[32,4,1,8,128]{4,3,1,0,2:T(8,128)} %get-tuple-element.16) | copy-start | bytes 1572868
  148.6 6.4 %copy-start.3 = (f32[32,4,1,8,4]{3,4,1,0,2:T(4,128)S(1)}, f32[32,4,1,8,4]{3,4,1,0,2:T(4,128)}, u32[]{:S(2)}) copy-start(f32[32,4,1,8,4]{3,4,1,0,2:T(4,128)} %get-tuple-element.14) | copy-start | bytes 49156
  148.6 7.0 %copy-start.4 = (bf16[2048,1,1,128]{3,2,0,1:T(2,128)(2,1)S(1)}, bf16[2048,1,1,128]{3,2,0,1:T(2,128)(2,1)}, u32[]{:S(2)}) copy-start(bf16[2048,1,1,128]{3,2,0,1:T(2,128)(2,1)} %get-tuple-element.7) | copy-start | bytes 1572868
  155.6 5.1 %copy-start.2 = (bf16[32,128,256]{1,2,0:T(8,128)(2,1)S(1)}, bf16[32,128,256]{1,2,0:T(8,128)(2,1)}, u32[]{:S(2)}) copy-start(bf16[32,128,256]{1,2,0:T(8,128)(2,1)} %copy.64) | copy-start | bytes 6291460
  162.3 102.0 %reduce-scatter.2.cloned.1.call-start = ((), (), s32[]{:S(2)}) async-start(), calls=%async_computation.5 | async-start | bytes 2359296 | tf_op jit(solution)/shard_map/reduce_scatter | solution.py:132
Sparse Core Ops, SparseCore 0:
  9.1 97.0 all-gather.2
  162.4 53.2 all-gather.4
  221.7 42.5 reduce-scatter.1
where the time goes:
time: 271 us
  waiting for transfers between devices  188 us (69%)
  matrix products  27.3 us (10%)
  starting transfers between devices  15.3 us (6%)
  other arithmetic  15.1 us (6%)
  between operations  13.3 us (5%)
  local copies, waits for them, and re-layouts  11.8 us (4%)
    all_gather x1, waiting for transfers between devices, on_device(): shard_piece = lax.all_gather(prompt, 'tp', axis=1, tiled=True)  82 us
    all_gather x1, waiting for transfers between devices, on_device(): lax.all_gather(attention, 'seq', axis=0, tiled=True)  53.3 us
    reduce_scatter x1, waiting for transfers between devices, on_device(): lax.psum_scatter(head_terms.astype(jnp.bfloat16), 'tp', scatter_dimension...  42.8 us
    all_to_all x1, waiting for transfers between devices, on_device(): lax.all_to_all(send_kv, ('grp', 'seq'), split_axis=0, concat_axis=0, tile...  9.17 us
    all_to_all x1, starting transfers between devices, on_device(): lax.all_to_all(send_rows, ('grp', 'seq'), split_axis=0, concat_axis=0, ti...  7.62 us
    all_to_all x1, starting transfers between devices, on_device(): lax.all_to_all(send_kv, ('grp', 'seq'), split_axis=0, concat_axis=0, tile...  7.41 us
    reduce_sum x1, other arithmetic, on_device(): jnp.sum(w_sent, axis=-1)  5.9 us
    dot_general x1, matrix products, on_device(): jnp.dot(lax.all_gather(attention, 'seq', axis=0, tiled=True), w_out, pref...  5.86 us
  transfers between devices with their start and end apart: 5, of which 4 were waited for; matrix products, arithmetic and copies ran while one was open for 10% of the time, Pallas kernels for 0%

commit v1 on v0

--- a/solution.py
+++ b/solution.py
@@ -24,7 +24,10 @@
     features = w_kv.shape[0]
     columns = w_kv.shape[1]
     row_count = queries.shape[0]
-    shard_piece = lax.all_gather(prompt, "tp", axis=1, tiled=True)
+    size = lax.axis_size("tp")
+    pieces = jnp.stack([prompt for _ in range(size)])
+    pieces = lax.all_to_all(pieces, "tp", split_axis=0, concat_axis=0)
+    shard_piece = jnp.concatenate(pieces, axis=1)
     running = jnp.dot(shard_piece, w_kv, preferred_element_type=jnp.float32)
     widened = shard_piece.astype(jnp.float32)
     squares = jnp.sum(widened * widened, axis=1)

time: 271 us -> 379 us (1.40)
  waiting for transfers between devices: 188 us -> 283 us
  starting transfers between devices: 15.3 us -> 23.8 us
  local copies, waits for them, and re-layouts: 11.8 us -> 16.1 us
    all_to_all x0 -> x1, waiting for transfers between devices: none -> 181 us  [on_device(): pieces = lax.all_to_all(pieces, 'tp', split_axis=0, concat_axis=0)]
    all_gather x1 -> x0, waiting for transfers between devices: 82 us -> none  [on_device(): shard_piece = lax.all_gather(prompt, 'tp', axis=1, tiled=True)]
    all_to_all x0 -> x1, starting transfers between devices: none -> 8.6 us  [on_device(): pieces = lax.all_to_all(pieces, 'tp', split_axis=0, concat_axis=0)]
    another operation x1 -> x2, local copies, waits for them, and re-layouts: 1.05 us -> 4.99 us  [the longest x1 3.94 us: on_device(): pieces = jnp.stack([prompt for _ in range(size)])]
  transfers between devices with their start and end apart: 5 -> 5, of which waited for: 4 -> 4; matrix products, arithmetic and copies ran while one was open for 10% -> 6% of each run, Pallas kernels for 0% -> 0%
where the time goes in v1:
time: 379 us; the launch traced here: 378 us
  waiting for transfers between devices  283 us (75%)
  matrix products  28.5 us (8%)
  starting transfers between devices  23.8 us (6%)
  local copies, waits for them, and re-layouts  16.1 us (4%)
  between operations  13.7 us (4%)
  other arithmetic  12.6 us (3%)
    all_to_all x1, waiting for transfers between devices, on_device(): pieces = lax.all_to_all(pieces, 'tp', split_axis=0, concat_axis=0)  181 us
    all_gather x1, waiting for transfers between devices, on_device(): lax.all_gather(attention, 'seq', axis=0, tiled=True)  50.8 us
    reduce_scatter x1, waiting for transfers between devices, on_device(): lax.psum_scatter(head_terms.astype(jnp.bfloat16), 'tp', scatter_dimension...  42.6 us
    all_to_all x1, waiting for transfers between devices, on_device(): lax.all_to_all(send_kv, ('grp', 'seq'), split_axis=0, concat_axis=0, tile...  9.2 us
    all_to_all x1, starting transfers between devices, on_device(): pieces = lax.all_to_all(pieces, 'tp', split_axis=0, concat_axis=0)  8.6 us
    all_to_all x1, starting transfers between devices, on_device(): lax.all_to_all(send_rows, ('grp', 'seq'), split_axis=0, concat_axis=0, ti...  7.62 us
  transfers between devices with their start and end apart: 5, of which 4 were waited for; matrix products, arithmetic and copies ran while one was open for 6% of the time, Pallas kernels for 0%

profile of v1, /device:TPU:2, one launch (start us, length us, event | category | flops | bytes accessed | tf_op | source)
XLA Modules:
  0.0 378.0 jit_solution(4311334833487350173)
XLA Ops:
  6.5 1.6 copy.71
  8.1 3.9 %stack.2 = bf16[8,512,1024]{1,2,0:T(8,128)(2,1)} broadcast(bf16[512,1024]{0,1:T(8,128)(2,1)S(1)} %copy.71), dimensions={1,2} | broadcast | bytes 9437184 | tf_op jit(solution)/shard_map/stack | solution.py:28
  12.1 8.6 %all-to-all-start.1 = ((bf16[8,512,1024]{1,2,0:T(8,128)(2,1)}), bf16[8,512,1024]{1,2,0:T(8,128)(2,1)}, u32[]{:S(2)}, u32[]{:S(2)}) async-start(bf16[8,512,1024]{1,2,0:T(8,128)(2,1)} %stack.2), calls=%async_computation.1 | async-start | bytes 16777216 | tf_op jit(solution)/shard_map/all_to_all | solution.py:29
  21.6 0.7 sub.35
  22.3 1.1 reshape.231
  23.4 2.9 copy.67
  26.7 180.6 %all-to-all-done.1 = bf16[8,512,1024]{1,2,0:T(8,128)(2,1)} async-done(((bf16[8,512,1024]{1,2,0:T(8,128)(2,1)}), bf16[8,512,1024]{1,2,0:T(8,128)(2,1)}, u32[]{:S(2)}, u32[]{:S(2)}) %all-to-all-start.1) | async-done | bytes 8388640 | tf_op jit(solution)/shard_map/all_to_all | solution.py:29
  207.3 7.6 %all-to-all-start = ((s32[32,1,8]{2,1,0:T(1,128)}), s32[32,1,8]{2,1,0:T(1,128)S(1)}, u32[]{:S(2)}, u32[]{:S(2)}) async-start(s32[32,1,8]{2,1,0:T(1,128)} %bitcast.10), calls=%async_computation | async-start | bytes 32768 | tf_op jit(solution)/shard_map/all_to_all | solution.py:56
  214.9 5.3 %multiply_reduce_fusion = f32[512]{0:T(512)S(1)} fusion(bf16[8,512,1024]{1,2,0:T(8,128)(2,1)} %all-to-all-done.1), kind=kLoop, calls=%fused_computation | loop fusion | flops 12582400 | bytes 8390656 | tf_op jit(solution)/shard_map/reduce_sum | solution.py:33
  220.3 5.8 %fusion.17 = bf16[512,256]{1,0:T(8,128)(2,1)S(1)} fusion(bf16[512,8192]{0,1:T(8,128)(2,1)} %bitcast.13, bf16[8192,256]{1,0:T(8,128)(2,1)S(1)} %copy-done.1, f32[512]{0:T(512)S(1)} %add_rsqrt_fusion), kind=kOutput, calls=%fused_computation.24 | convolution fusion | flops 2147745792 | bytes 12847104 | tf_op jit(solution)/shard_map/dot_general | solution.py:31
  226.7 1.3 copy.72
  228.0 7.4 %all-to-all-start.2 = ((bf16[32,8,8,256]{3,2,1,0:T(8,128)(2,1)}), bf16[32,8,8,256]{3,2,1,0:T(8,128)(2,1)S(1)}, u32[]{:S(2)}, u32[]{:S(2)}) async-start(bf16[32,8,8,256]{3,2,1,0:T(8,128)(2,1)} %copy.72), calls=%async_computation.2 | async-start | bytes 2097152 | tf_op jit(solution)/shard_map/all_to_all | solution.py:55
  235.6 2.6 fusion.37
  238.2 3.0 fusion.38
  241.5 9.2 %all-to-all-done.2 = bf16[32,8,8,256]{3,2,1,0:T(8,128)(2,1)S(1)} async-done(((bf16[32,8,8,256]{3,2,1,0:T(8,128)(2,1)}), bf16[32,8,8,256]{3,2,1,0:T(8,128)(2,1)S(1)}, u32[]{:S(2)}, u32[]{:S(2)}) %all-to-all-start.2) | async-done | bytes 1048608 | tf_op jit(solution)/shard_map/all_to_all | solution.py:55
  251.0 2.3 fusion.34
  253.3 4.6 %fusion.2 = (f32[32,4,8]{0,2,1:T(8,128)S(1)}, f32[2048,32,4,8]{0,1,3,2:T(8,128)}) fusion(pred[32,2048]{1,0:T(8,128)(4,1)S(1)} %iota_compare_fusion, bf16[32,4,8,128]{3,2,1,0:T(8,128)(2,1)S(1)} %reshape.231, bf16[2048,1,1,128]{3,2,0,1:T(2,128)(2,1)S(1)} %get-tuple-element.8), kind=kOutput, calls=%fused_computation.5 | convolution fusion | flops 543161344 | bytes 9244672 | tf_op jit(solution)/shard_map/rinhd,knd->rinhk/dot_general | solution.py:81
  258.1 5.9 %fusion = (f32[32,4,8]{0,2,1:T(8,128)S(1)}, bf16[32,4,8,2048]{3,0,2,1:T(8,128)(2,1)}) fusion(f32[2048,32,4,8]{0,1,3,2:T(8,128)} %get-tuple-element.18, f32[32,4,8]{0,2,1:T(8,128)S(1)} %copy.81, pred[32,2048]{1,0:T(8,128)(4,1)S(1)} %iota_compare_fusion), kind=kLoop, calls=%fused_computation.3 | loop fusion | flops 10484736 | bytes 12656640 | tf_op jit(solution)/shard_map/reduce_sum | solution.py:105
  265.1 5.1 %fusion.13 = f32[32,4,1,8,128]{4,3,1,0,2:T(8,128)S(1)} fusion(bf16[32,4,8,2048]{3,0,2,1:T(8,128)(2,1)} %get-tuple-element.6, bf16[2048,1,1,128]{3,2,0,1:T(2,128)(2,1)S(1)} %copy-done.5), kind=kOutput, calls=%fused_computation.21 | convolution fusion | flops 536870912 | bytes 5242880 | tf_op jit(solution)/shard_map/rinhk,knd->rinhd/dot_general | solution.py:113
  270.3 0.7 fusion.16
  271.0 0.8 copy.124
  271.8 50.8 %all-gather.2.cloned.1.call-done = bf16[2048,1024]{1,0:T(8,128)(2,1)} async-done(((bf16[128,1024]{1,0:T(8,128)(2,1)}), bf16[2048,1024]{1,0:T(8,128)(2,1)}) %all-gather.2.cloned.1.call-update) | async-done | bytes 4194320 | tf_op jit(solution)/shard_map/all_gather | solution.py:131
  322.7 5.8 %convolution_convert_fusion = bf16[2048,512]{1,0:T(8,128)(2,1)} fusion(bf16[2048,1024]{1,0:T(8,128)(2,1)} %all-gather.2.cloned.1.call-done, bf16[1024,512]{1,0:T(8,128)(2,1)S(1)} %copy-done), kind=kOutput, calls=%fused_computation.9 | convolution fusion | flops 2148532224 | bytes 7340032 | tf_op jit(solution)/shard_map/dot_general | solution.py:130
  328.5 42.6 %reduce-scatter.2.cloned.1.call-done = bf16[256,512]{1,0:T(8,128)(2,1)} async-done(((bf16[2048,512]{1,0:T(8,128)(2,1)}), bf16[256,512]{1,0:T(8,128)(2,1)}) %reduce-scatter.2.cloned.1.call-update) | async-done | bytes 262160 | tf_op jit(solution)/shard_map/reduce_scatter | solution.py:135
  (67 shorter events, 4.0 us)
Async XLA Ops:
  6.5 316.1 %copy-start = (bf16[1024,512]{1,0:T(8,128)(2,1)S(1)}, bf16[1024,512]{1,0:T(8,128)(2,1)}, u32[]{:S(2)}) copy-start(bf16[1024,512]{1,0:T(8,128)(2,1)} %param.19) | copy-start | bytes 3145732
  12.1 8.6 %copy-start.11 = (s32[64,1]{0,1:T(1,128)S(1)}, s32[64,1]{0,1:T(1,128)}, u32[]{:S(2)}) copy-start(s32[64,1]{0,1:T(1,128)} %param.12) | copy-start | bytes 772
  12.1 9.0 %copy-start.14 = (s32[64]{0:T(128)S(1)}, s32[64]{0:T(128)}, u32[]{:S(2)}) copy-start(s32[64]{0:T(128)} %param.13) | copy-start | bytes 772
  12.1 11.3 %copy-start.2 = (bf16[32,128,256]{2,1,0:T(8,128)(2,1)S(1)}, bf16[32,128,256]{2,1,0:T(8,128)(2,1)}, u32[]{:S(2)}) copy-start(bf16[32,128,256]{2,1,0:T(8,128)(2,1)} %param.16) | copy-start | bytes 6291460
  12.1 195.2 %all-to-all-start.1 = ((bf16[8,512,1024]{1,2,0:T(8,128)(2,1)}), bf16[8,512,1024]{1,2,0:T(8,128)(2,1)}, u32[]{:S(2)}, u32[]{:S(2)}) async-start(bf16[8,512,1024]{1,2,0:T(8,128)(2,1)} %stack.2), calls=%async_computation.1 | async-start | bytes 16777216 | tf_op jit(solution)/shard_map/all_to_all | solution.py:29
  20.7 5.6 %copy-start.10 = (f32[32,8,2]{0,2,1:T(2,128)S(1)}, f32[32,8,2]{0,2,1:T(2,128)}, u32[]{:S(2)}) copy-start(f32[32,8,2]{0,2,1:T(2,128)} %param.17) | copy-start | bytes 6148
  20.7 5.6 %copy-start.7 = (bf16[32,4,256]{2,1,0:T(4,128)(2,1)S(1)}, bf16[32,4,256]{2,1,0:T(4,128)(2,1)}, u32[]{:S(2)}) copy-start(bf16[32,4,256]{2,1,0:T(4,128)(2,1)} %param.15) | copy-start | bytes 196612
  20.7 5.8 %copy-start.15 = (s32[32]{0:T(128)S(1)}, s32[32]{0:T(128)}, u32[]{:S(2)}) copy-start(s32[32]{0:T(128)} %param.18) | copy-start | bytes 388
  21.1 0.5 copy-start.12
  207.3 20.7 %all-to-all-start = ((s32[32,1,8]{2,1,0:T(1,128)}), s32[32,1,8]{2,1,0:T(1,128)S(1)}, u32[]{:S(2)}, u32[]{:S(2)}) async-start(s32[32,1,8]{2,1,0:T(1,128)} %bitcast.10), calls=%async_computation | async-start | bytes 32768 | tf_op jit(solution)/shard_map/all_to_all | solution.py:56
  214.9 5.3 %copy-start.1 = (bf16[8192,256]{1,0:T(8,128)(2,1)S(1)}, bf16[8192,256]{1,0:T(8,128)(2,1)}, u32[]{:S(2)}) copy-start(bf16[8192,256]{1,0:T(8,128)(2,1)} %param.11) | copy-start | bytes 12582916
  220.3 5.9 %copy-start.13 = (s32[64]{0:T(128)S(1)}, s32[64]{0:T(128)}, u32[]{:S(2)}) copy-start(s32[64]{0:T(128)} %copy-done.12) | copy-start | bytes 772
  228.0 22.7 %all-to-all-start.2 = ((bf16[32,8,8,256]{3,2,1,0:T(8,128)(2,1)}), bf16[32,8,8,256]{3,2,1,0:T(8,128)(2,1)S(1)}, u32[]{:S(2)}, u32[]{:S(2)}) async-start(bf16[32,8,8,256]{3,2,1,0:T(8,128)(2,1)} %copy.72), calls=%async_computation.2 | async-start | bytes 2097152 | tf_op jit(solution)/shard_map/all_to_all | solution.py:55
  235.4 87.3 %all-gather.2.cloned.1.call-start = ((), (), s32[]{:S(2)}) async-start(), calls=%async_computation.4 | async-start | bytes 4456448 | tf_op jit(solution)/shard_map/all_gather | solution.py:131
  253.3 4.7 %copy-start.8 = (f32[32,4,8]{2,1,0:T(4,128)S(1)}, f32[32,4,8]{2,1,0:T(4,128)}, u32[]{:S(2)}) copy-start(f32[32,4,8]{2,1,0:T(4,128)} %get-tuple-element.13) | copy-start | bytes 12292
  253.3 4.7 %copy-start.9 = (f32[32,4,8]{2,1,0:T(4,128)S(1)}, f32[32,4,8]{2,1,0:T(4,128)}, u32[]{:S(2)}) copy-start(f32[32,4,8]{2,1,0:T(4,128)} %get-tuple-element.15) | copy-start | bytes 12292
  258.1 6.0 %copy-start.6 = (f32[32,4,1,8,128]{4,3,1,0,2:T(8,128)S(1)}, f32[32,4,1,8,128]{4,3,1,0,2:T(8,128)}, u32[]{:S(2)}) copy-start(f32[32,4,1,8,128]{4,3,1,0,2:T(8,128)} %get-tuple-element.16) | copy-start | bytes 1572868
  258.1 6.5 %copy-start.4 = (f32[32,4,1,8,4]{3,4,1,0,2:T(4,128)S(1)}, f32[32,4,1,8,4]{3,4,1,0,2:T(4,128)}, u32[]{:S(2)}) copy-start(f32[32,4,1,8,4]{3,4,1,0,2:T(4,128)} %get-tuple-element.14) | copy-start | bytes 49156
  258.1 7.0 %copy-start.5 = (bf16[2048,1,1,128]{3,2,0,1:T(2,128)(2,1)S(1)}, bf16[2048,1,1,128]{3,2,0,1:T(2,128)(2,1)}, u32[]{:S(2)}) copy-start(bf16[2048,1,1,128]{3,2,0,1:T(2,128)(2,1)} %get-tuple-element.7) | copy-start | bytes 1572868
  265.1 5.1 %copy-start.3 = (bf16[32,128,256]{1,2,0:T(8,128)(2,1)S(1)}, bf16[32,128,256]{1,2,0:T(8,128)(2,1)}, u32[]{:S(2)}) copy-start(bf16[32,128,256]{1,2,0:T(8,128)(2,1)} %copy.67) | copy-start | bytes 6291460
  271.8 99.4 %reduce-scatter.2.cloned.1.call-start = ((), (), s32[]{:S(2)}) async-start(), calls=%async_computation.5 | async-start | bytes 2359296 | tf_op jit(solution)/shard_map/reduce_scatter | solution.py:135
Sparse Core Ops, SparseCore 0:
  271.9 50.7 all-gather.1
  328.7 42.4 reduce-scatter.1
